TPU v7x, 32 devices: a whole 2x2x4 slice. The times are simulated.
32 devices in a mesh: blk: 8 (over z, y), col: 4 (over x, core).
Axes of the slice: x: 2, y: 2, z: 4, core: 2. Of those that a mesh axis runs over, the one named last changes fastest.
Arguments:
- amplitudes: float32 [800, 32, 1601], P('col', 'blk'), may hold values from -6 to 6
- integrals: float32 [2, 1024, 20, 1601], P(None, 'blk', 'col'), may hold values from -0.03125 to 0.03125
- block_ids: int32 [20], replicated, may hold values from 0 to 799, as said below
- mirror: int32 [16], replicated, may hold values from 0 to 15, each once
Outputs:
- ladder_residual: float32 [16, 1024], P('col', 'blk')
Inputs may be any that keep to these rules, and one draw needn't show every extreme that they name: `block_ids`: 20 distinct folded block numbers; 0 and 799 are always among them. `mirror`: a permutation of the slab positions.
All inputs are finite; a program needn't handle non-finite values.
Results may differ from a plain program's by a relative error of at most 0.000073.
Values sent between devices are 32-bit elements; how exact they have to be, the bound alone decides.
A program may use at most 64 MiB of HBM per device.

v0:
```python
import jax
import jax.numpy as jnp
from jax import lax
from jax.sharding import PartitionSpec as P


def body(amplitudes, integrals, block_ids, mirror):
    blocks_here = amplitudes.shape[0]
    block_width = amplitudes.shape[2]
    owned_count = integrals.shape[2]
    local_rows = integrals.shape[1]
    block_base = lax.axis_index("col") * blocks_here
    stacked = integrals.reshape(2 * local_rows, owned_count, block_width)
    wanted = block_ids - block_base
    onehot = (wanted[:, None] == jnp.arange(blocks_here, dtype=jnp.int32)[None, :]).astype(
        jnp.float32
    )
    selected = lax.psum_scatter(
        jnp.einsum("kh,hrl->krl", onehot, amplitudes, precision=lax.Precision.HIGHEST),
        "col",
        scatter_dimension=0,
        tiled=True,
    )
    products = jnp.einsum(
        "kcl,wkl->cw",
        lax.all_gather(selected, "blk", axis=1, tiled=True),
        stacked,
        precision=lax.Precision.HIGHEST,
    )
    pair_count = products.shape[0] // 2
    plus_part = products[:, :local_rows]
    minus_part = products[:, local_rows:]
    direct = 0.5 * (
        plus_part[:pair_count]
        + minus_part[:pair_count]
        + plus_part[pair_count:]
        - minus_part[pair_count:]
    )
    swapped = 0.5 * (
        plus_part[:pair_count]
        - minus_part[:pair_count]
        + plus_part[pair_count:]
        + minus_part[pair_count:]
    )
    direct_sum, swapped_sum = (
        lax.psum_scatter(direct, "col", scatter_dimension=0, tiled=True),
        lax.psum_scatter(swapped, "col", scatter_dimension=0, tiled=True),
    )
    swapped_all = lax.all_gather(swapped_sum, "col", axis=0, tiled=True)
    own_pairs = direct_sum.shape[0]
    targets = lax.dynamic_slice_in_dim(mirror, lax.axis_index("col") * own_pairs, own_pairs)
    pick = (targets[:, None] == jnp.arange(pair_count, dtype=jnp.int32)[None, :]).astype(
        jnp.float32
    )
    return direct_sum + jnp.dot(pick, swapped_all, precision=lax.Precision.HIGHEST)


def solution(mesh):
    in_specs = (P("col", "blk", None), P(None, "blk", "col", None), P(), P())
    out_specs = P("col", "blk")
    return jax.shard_map(body, mesh=mesh, in_specs=in_specs, out_specs=out_specs, check_vma=False)
```

profile of v0, /device:TPU:0, one launch (start us, length us, event | category | flops | bytes accessed | tf_op | source)
XLA Modules:
  0.0 118.5 jit_solution(15536446643626224223)
XLA Ops:
  6.5 0.0 copy-start.1
  6.5 0.0 all-reduce.6.cloned.1.call-start
  6.5 0.7 broadcast_subtract_fusion
  7.2 4.3 %fusion = f32[20,4,1601]{2,0,1:T(8,128)S(1)} fusion(f32[200,4,1601]{2,1,0:T(4,128)} %param.4, s32[20]{0:T(128)S(1)} %broadcast_subtract_fusion), kind=kOutput, calls=%fused_computation | convolution fusion | flops 307396000 | bytes 5635600 | tf_op jit(solution)/shard_map/kh,hrl->krl/dot_general | solution.py:19
  11.6 1.0 copy.8
  12.6 0.0 all-reduce.6.cloned.1.call-update
  12.6 0.0 copy-done.1
  12.6 0.6 dynamic-slice
  14.5 0.0 copy-start
  14.5 10.6 %reshape.5 = f32[256,5,1601]{0,2,1:T(8,128)} reshape(f32[2,128,5,1601]{1,0,3,2:T(2,128)} %param.5) | data formatting | bytes 16394240 | tf_op jit(solution)/shard_map/reshape | solution.py:13
  25.1 0.0 copy-done
  25.1 0.1 dynamic_slice.3
  25.2 23.6 %all-reduce.6.cloned.1.call-done = f32[20,4,1601]{2,1,0:T(4,128)} async-done(((f32[20,4,1601]{2,1,0:T(4,128)}), f32[20,4,1601]{2,1,0:T(4,128)}) %all-reduce.6.cloned.1.call-update) | async-done | bytes 512336
  48.8 0.9 constant_dynamic-slice_fusion
  49.7 38.5 %all_gather.6 = f32[5,32,1601]{2,0,1:T(8,128)S(1)} all-gather(f32[5,4,1601]{2,0,1:T(8,128)S(1)} %copy.5), channel_id=1, replica_groups=mesh['blk'=8,'col'=4] {'blk'}, dimensions={1}, use_global_device_ids=true | all-gather | bytes 1152720 | tf_op jit(solution)/shard_map/all_gather | solution.py:26
  88.3 7.3 %convolution_bitcast_fusion = f32[32,256]{1,0:T(8,128)S(1)} fusion(f32[256,5,1601]{0,2,1:T(8,128)} %reshape.5, f32[5,32,1601]{2,0,1:T(8,128)S(1)} %all_gather.6), kind=kOutput, calls=%fused_computation.2 | convolution fusion | flops 786923520 | bytes 9254528 | tf_op jit(solution)/shard_map/kcl,wkl->cw/dot_general | solution.py:24
  95.6 10.1 %all-reduce.3 = (f32[16,128]{1,0:T(8,128)S(1)}, f32[16,128]{1,0:T(8,128)S(1)}) all-reduce(f32[16,128]{1,0:T(8,128)S(1)} %get-tuple-element.8, f32[16,128]{1,0:T(8,128)S(1)} %get-tuple-element.7), channel_id=4, replica_groups=mesh['blk'=8,'col'=4] {'col'}, use_global_device_ids=true, to_apply=%region_2.0.clone | all-reduce | flops 4096 | bytes 32768
  105.7 5.2 %all-gather = f32[4,4,128]{2,1,0:T(4,128)S(1)} all-gather(f32[1,4,128]{2,1,0:T(4,128)S(1)} %dynamic-slice_bitcast_fusion), channel_id=1, replica_groups=mesh['blk'=8,'col'=4] {'col'}, dimensions={0}, use_global_device_ids=true | all-gather | bytes 10240 | tf_op jit(solution)/shard_map/all_gather | solution.py:49
  110.9 0.8 convolution_add_fusion
  (3 shorter events, 0.0 us)
Async XLA Ops:
  6.5 6.1 %copy-start.1 = (u32[32]{0:T(128)S(1)}, u32[32]{0:T(128)}, u32[]{:S(2)}) copy-start(u32[32]{0:T(128)} %constant.18) | copy-start | bytes 388
  6.5 42.3 %all-reduce.6.cloned.1.call-start = ((), (), s32[]{:S(2)}) async-start(), calls=%async_computation | async-start | bytes 1064960
  14.5 10.7 %copy-start = (s32[16]{0:T(128)S(1)}, s32[16]{0:T(128)}, u32[]{:S(2)}) copy-start(s32[16]{0:T(128)} %param.7) | copy-start | bytes 196
Sparse Core Ops, SparseCore 0:
  12.7 36.0 all-reduce.5
where the time goes:
time: 119 us
  blocking collectives  53.9 us (45%)
  waiting for transfers between devices  23.6 us (20%)
  between operations  14.7 us (12%)
  local copies, waits for them, and re-layouts  13.3 us (11%)
  matrix products  12.4 us (10%)
    all_gather x1, blocking collectives, body(): lax.all_gather(selected, 'blk', axis=1, tiled=True)  38.5 us
    unnamed x2, waiting for transfers between devices  23.6 us
    reshape x1, local copies, waits for them, and re-layouts, body(): stacked = integrals.reshape(2 * local_rows, owned_count, block_width)  10.6 us
    unnamed x1, blocking collectives  10.1 us
    dot_general x1, matrix products, body(): jnp.einsum('kcl,wkl->cw', lax.all_gather(selected, 'blk', axis=1, tiled=T...  7.29 us
    all_gather x1, blocking collectives, body(): swapped_all = lax.all_gather(swapped_sum, 'col', axis=0, tiled=True)  5.19 us
    dot_general x1, matrix products, body(): jnp.einsum('kh,hrl->krl', onehot, amplitudes, precision=lax.Precision.HIG...  4.35 us
  transfers between devices with their start and end apart: 1, of which 1 were waited for; matrix products, arithmetic and copies ran while one was open for 10% of the time, Pallas kernels for 0%

commit v1 on v0

--- a/solution.py
+++ b/solution.py
@@ -23,7 +23,7 @@
     )
     products = jnp.einsum(
         "kcl,wkl->cw",
-        lax.all_gather(selected, "blk", axis=1, tiled=True),
+        jnp.concatenate(lax.all_gather(selected, "blk"), 1),
         stacked,
         precision=lax.Precision.HIGHEST,
     )

time: 119 us -> 115 us (0.966)
  blocking collectives: 53.9 us -> 49.5 us
    all_gather x1, blocking collectives: 38.5 us -> 33.8 us  [body(): lax.all_gather(selected, 'blk')]
where the time goes in v1:
time: 115 us; the launch traced here: 114 us
  blocking collectives  49.5 us (43%)
  waiting for transfers between devices  23.6 us (21%)
  between operations  14.7 us (13%)
  local copies, waits for them, and re-layouts  13.7 us (12%)
  matrix products  12.2 us (11%)
    all_gather x1, blocking collectives, body(): lax.all_gather(selected, 'blk')  33.8 us
    unnamed x2, waiting for transfers between devices  23.6 us
    reshape x1, local copies, waits for them, and re-layouts, body(): stacked = integrals.reshape(2 * local_rows, owned_count, block_width)  10.6 us
    unnamed x1, blocking collectives  10.5 us
    dot_general x1, matrix products, body(): jnp.einsum('kcl,wkl->cw', jnp.concatenate(lax.all_gather(selected, 'blk')...  7.1 us
    all_gather x1, blocking collectives, body(): swapped_all = lax.all_gather(swapped_sum, 'col', axis=0, tiled=True)  5.19 us
    dot_general x1, matrix products, body(): jnp.einsum('kh,hrl->krl', onehot, amplitudes, precision=lax.Precision.HIG...  4.35 us
  transfers between devices with their start and end apart: 1, of which 1 were waited for; matrix products, arithmetic and copies ran while one was open for 10% of the time, Pallas kernels for 0%

profile of v1, /device:TPU:0, one launch (start us, length us, event | category | flops | bytes accessed | tf_op | source)
XLA Modules:
  0.0 114.4 jit_solution(7860244013937841792)
XLA Ops:
  6.5 0.0 copy-start.1
  6.5 0.0 all-reduce.6.cloned.1.call-start
  6.5 0.7 broadcast_subtract_fusion
  7.2 4.3 %fusion = f32[20,4,1601]{2,0,1:T(8,128)S(1)} fusion(f32[200,4,1601]{2,1,0:T(4,128)} %param.4, s32[20]{0:T(128)S(1)} %broadcast_subtract_fusion), kind=kOutput, calls=%fused_computation | convolution fusion | flops 307396000 | bytes 5635600 | tf_op jit(solution)/shard_map/kh,hrl->krl/dot_general | solution.py:19
  11.6 1.0 copy.11
  12.6 0.0 all-reduce.6.cloned.1.call-update
  12.6 0.0 copy-done.1
  12.6 0.6 dynamic-slice
  14.5 0.0 copy-start
  14.5 10.6 %reshape.13 = f32[256,5,1601]{0,2,1:T(8,128)} reshape(f32[2,128,5,1601]{1,0,3,2:T(2,128)} %param.5) | data formatting | bytes 16394240 | tf_op jit(solution)/shard_map/reshape | solution.py:13
  25.1 0.0 copy-done
  25.1 0.1 dynamic_slice.3
  25.2 23.6 %all-reduce.6.cloned.1.call-done = f32[20,4,1601]{2,1,0:T(4,128)} async-done(((f32[20,4,1601]{2,1,0:T(4,128)}), f32[20,4,1601]{2,1,0:T(4,128)}) %all-reduce.6.cloned.1.call-update) | async-done | bytes 512336
  48.8 0.9 constant_dynamic-slice_fusion
  49.7 33.8 %all-gather = f32[40,4,1601]{2,1,0:T(4,128)S(1)} all-gather(f32[5,4,1601]{2,1,0:T(4,128)S(1)} %constant_dynamic-slice_fusion), channel_id=2, replica_groups=mesh['blk'=8,'col'=4] {'blk'}, dimensions={0}, use_global_device_ids=true | all-gather | bytes 1152720 | tf_op jit(solution)/shard_map/all_gather | solution.py:26
  83.5 0.1 copy.12
  83.6 0.4 reshape.12
  84.0 7.1 %convolution_bitcast_fusion = f32[32,256]{1,0:T(8,128)S(1)} fusion(f32[5,32,1601]{2,1,0:T(8,128)S(1)} %reshape.12, f32[256,5,1601]{0,2,1:T(8,128)} %reshape.13), kind=kOutput, calls=%fused_computation.2 | convolution fusion | flops 786923520 | bytes 9254528 | tf_op jit(solution)/shard_map/kcl,wkl->cw/dot_general | solution.py:24
  91.1 10.5 %all-reduce.3 = (f32[16,128]{1,0:T(8,128)S(1)}, f32[16,128]{1,0:T(8,128)S(1)}) all-reduce(f32[16,128]{1,0:T(8,128)S(1)} %get-tuple-element.8, f32[16,128]{1,0:T(8,128)S(1)} %get-tuple-element.7), channel_id=5, replica_groups=mesh['blk'=8,'col'=4] {'col'}, use_global_device_ids=true, to_apply=%region_2.0.clone | all-reduce | flops 4096 | bytes 32768
  101.6 5.2 %all-gather.1 = f32[4,4,128]{2,1,0:T(4,128)S(1)} all-gather(f32[1,4,128]{2,1,0:T(4,128)S(1)} %dynamic-slice_bitcast_fusion), channel_id=1, replica_groups=mesh['blk'=8,'col'=4] {'col'}, dimensions={0}, use_global_device_ids=true | all-gather | bytes 10240 | tf_op jit(solution)/shard_map/all_gather | solution.py:49
  106.8 0.8 convolution_add_fusion
  (2 shorter events, 0.0 us)
Async XLA Ops:
  6.5 6.1 %copy-start.1 = (u32[32]{0:T(128)S(1)}, u32[32]{0:T(128)}, u32[]{:S(2)}) copy-start(u32[32]{0:T(128)} %constant.18) | copy-start | bytes 388
  6.5 42.3 %all-reduce.6.cloned.1.call-start = ((), (), s32[]{:S(2)}) async-start(), calls=%async_computation | async-start | bytes 1064960
  14.5 10.7 %copy-start = (s32[16]{0:T(128)S(1)}, s32[16]{0:T(128)}, u32[]{:S(2)}) copy-start(s32[16]{0:T(128)} %param.7) | copy-start | bytes 196
Sparse Core Ops, SparseCore 0:
  12.7 36.0 all-reduce.5
